TPU v7x, 32 devices: a whole 2x2x4 slice. The times are simulated.
32 devices in a mesh: seg: 8 (over z, core), seq: 4 (over y, x).
Axes of the slice: x: 2, y: 2, z: 4, core: 2. Of those that a mesh axis runs over, the one named last changes fastest.
Arguments:
- layer_input: bfloat16 [8, 2048, 1024], P('seg', 'seq'), may hold values from -6 to 6
- output_grad: bfloat16 [8, 2048, 1024], P('seg', 'seq'), may hold values from -6 to 6
- norm1_gain: float32 [1024], replicated, may hold values from 0.5 to 1.5
- norm2_gain: float32 [1024], replicated, may hold values from 0.5 to 1.5
- w_qkv: bfloat16 [1024, 3072], replicated, may hold values from -0.25 to 0.25
- w_out: bfloat16 [1024, 1024], replicated, may hold values from -0.75 to 0.75
- w_gate: bfloat16 [1024, 2816], replicated, may hold values from -0.1875 to 0.1875
- w_up: bfloat16 [1024, 2816], replicated, may hold values from -0.1875 to 0.1875
- w_down: bfloat16 [2816, 1024], replicated, may hold values from -0.109375 to 0.109375
- mem_keys: bfloat16 [8, 1024, 1024], P('seg', 'seq'), may hold values from -8 to 8
- mem_values: bfloat16 [8, 1024, 1024], P('seg', 'seq'), may hold values from -8 to 8
- memory_flags: int32 [8], replicated, may hold values from 0 to 1, as said below
- sources: int32 [8, 3], replicated, may hold values from 0 to 7, as said below
Outputs:
- output: bfloat16 [8, 2048, 1024], P('seg', 'seq')
- input_grad: float32 [8, 2048, 1024], P('seg', 'seq')
- grad_norm1: float32 [1024], P('seq')
- grad_norm2: float32 [1024], P('seq')
- grad_qkv: float32 [1024, 3072], P('seq')
- grad_out: float32 [1024, 1024], P('seq')
- grad_gate: float32 [1024, 2816], P('seq')
- grad_up: float32 [1024, 2816], P('seq')
- grad_down: float32 [2816, 1024], P('seq')
Inputs may be any that keep to these rules, and one draw needn't show every extreme that they name: `memory_flags`: exactly half of the segments have flag 1. `sources`: row s lists 3 different segments, none of them s. The first column is a permutation of the segments, and the first source of a segment has the other flag than the segment.
All inputs are finite; a program needn't handle non-finite values.
Results may differ from a plain program's by a relative error of at most 0.023.
Values may be sent and summed in bfloat16 or wider, within the bound.
A program may use at most 256 MiB of HBM per device.

v0:
```python
import jax
import jax.numpy as jnp
from jax import lax
from jax.sharding import PartitionSpec as P

D = 1024
HEADS = 8
HEAD_DIM = 128
masked_score = -1e30
epsilon = 1e-06
rotary_base = 10000.0


def product(former, latter):
    return jnp.dot(former, latter, preferred_element_type=jnp.float32)


def product_nt(former, latter):
    return lax.dot_general(
        former, latter, (((1,), (1,)), ((), ())), preferred_element_type=jnp.float32
    )


def product_tn(former, latter):
    return lax.dot_general(
        former, latter, (((0,), (0,)), ((), ())), preferred_element_type=jnp.float32
    )


def norm_forward(values, norm_gain):
    inverse = lax.rsqrt(jnp.mean(values * values, axis=-1, keepdims=True) + epsilon)
    return (values * inverse * norm_gain, inverse)


def norm_backward(values, inverse, norm_gain, upstream):
    weighted = upstream * norm_gain
    inner_mean = jnp.mean(weighted * values, axis=-1, keepdims=True)
    grad_values = inverse * weighted - inverse * inverse * inverse * values * inner_mean
    grad_gain = jnp.sum(upstream * values * inverse, axis=0)
    return (grad_values, grad_gain)


def turn_tables(positions):
    half_dim = HEAD_DIM // 2
    exponent = -2.0 * jnp.arange(half_dim, dtype=jnp.float32) / HEAD_DIM
    angles = positions[:, None] * jnp.power(rotary_base, exponent)[None, :]
    angles = jnp.concatenate([angles, angles], axis=1)
    return (jnp.cos(angles)[:, None, :], jnp.sin(angles)[:, None, :])


def rotate(matrix, cosine_table, sine_table, direction):
    row_count = matrix.shape[0]
    half_dim = HEAD_DIM // 2
    shaped = matrix.reshape(row_count, HEADS, HEAD_DIM)
    turned = jnp.concatenate([-shaped[..., half_dim:], shaped[..., :half_dim]], axis=-1)
    return (shaped * cosine_table + direction * turned * sine_table).reshape(
        row_count, HEADS * HEAD_DIM
    )


def on_device(
    layer_input,
    output_grad,
    norm1_gain,
    norm2_gain,
    w_qkv,
    w_out,
    w_gate,
    w_up,
    w_down,
    mem_keys,
    mem_values,
    memory_flags,
    sources,
):
    seg_index = lax.axis_index("seg")
    seq_index = lax.axis_index("seq")
    tokens = layer_input.shape[1]
    score_scale = HEAD_DIM ** (-0.5)
    flag_on = lax.dynamic_index_in_dim(memory_flags, seg_index, 0, keepdims=False) > 0
    listed = lax.dynamic_index_in_dim(sources, seg_index, 0, keepdims=False)
    picked = jnp.concatenate([jnp.reshape(seg_index, (1,)), listed])
    every_keys, every_values = (
        lax.all_gather(mem_keys, "seg", axis=0, tiled=True),
        lax.all_gather(mem_values, "seg", axis=0, tiled=True),
    )
    chosen_keys = jnp.take(every_keys, picked, axis=0)
    chosen_values = jnp.take(every_values, picked, axis=0)
    memory_keys, memory_values = (
        lax.all_gather(chosen_keys, "seq", axis=1, tiled=True),
        lax.all_gather(chosen_values, "seq", axis=1, tiled=True),
    )
    memory_key_blocks = memory_keys.reshape(-1, tokens, HEADS, HEAD_DIM)
    memory_value_blocks = memory_values.reshape(-1, tokens, HEADS, HEAD_DIM)
    memory_blocks = memory_key_blocks.shape[0]
    inputs = layer_input[0].astype(jnp.float32)
    first_norm, first_inverse = norm_forward(inputs, norm1_gain)
    first_low = first_norm.astype(jnp.bfloat16)
    projected = product(first_low, w_qkv)
    positions = seq_index * tokens + lax.iota(jnp.int32, tokens)
    cosine_table, sine_table = turn_tables(positions.astype(jnp.float32))
    queries = rotate(projected[:, :D], cosine_table, sine_table, 1.0).astype(jnp.bfloat16)
    own_keys = rotate(projected[:, D : 2 * D], cosine_table, sine_table, 1.0).astype(jnp.bfloat16)
    own_values = projected[:, 2 * D :].astype(jnp.bfloat16)
    all_keys, all_values = (
        lax.all_gather(own_keys, "seq", axis=0, tiled=True),
        lax.all_gather(own_values, "seq", axis=0, tiled=True),
    )
    key_blocks = all_keys.reshape(-1, tokens, HEADS, HEAD_DIM)
    value_blocks = all_values.reshape(-1, tokens, HEADS, HEAD_DIM)
    query_heads = queries.reshape(tokens, HEADS, HEAD_DIM)
    memory_open = jnp.broadcast_to(flag_on, (tokens, tokens))
    own_count = seq_index + 1
    key_offsets = lax.iota(jnp.int32, tokens)

    def own_open(block):
        return (block * tokens + key_offsets)[None, :] <= positions[:, None]

    def block_scores(key_block, open_mask):
        raw = (
            jnp.einsum("qhd,khd->hqk", query_heads, key_block, preferred_element_type=jnp.float32)
            * score_scale
        )
        return jnp.where(open_mask[None], raw, masked_score)

    def sweep(step, carry):

        def memory_turn(block, state):
            return step(
                state,
                block,
                memory_key_blocks[block],
                memory_value_blocks[block],
                memory_open,
                False,
            )

        def own_turn(block, state):
            return step(state, block, key_blocks[block], value_blocks[block], own_open(block), True)

        carry = lax.fori_loop(0, memory_blocks, memory_turn, carry)
        return lax.fori_loop(0, own_count, own_turn, carry)

    def max_step(carry, block, key_block, value_block, open_mask, own):
        row_max, row_sum = carry
        scores = block_scores(key_block, open_mask)
        new_max = jnp.maximum(row_max, jnp.max(scores, axis=2))
        row_sum = row_sum * jnp.exp(row_max - new_max) + jnp.sum(
            jnp.exp(scores - new_max[..., None]), axis=2
        )
        return (new_max, row_sum)

    start_max = jnp.full((HEADS, tokens), masked_score, jnp.float32)
    row_max, row_sum = sweep(max_step, (start_max, jnp.zeros((HEADS, tokens), jnp.float32)))
    log_totals = row_max + jnp.log(row_sum)

    def mix_step(total, block, key_block, value_block, open_mask, own):
        weights_low = jnp.exp(block_scores(key_block, open_mask) - log_totals[..., None]).astype(
            jnp.bfloat16
        )
        return total + jnp.einsum(
            "hqk,khd->qhd", weights_low, value_block, preferred_element_type=jnp.float32
        )

    attended = sweep(mix_step, jnp.zeros((tokens, HEADS, HEAD_DIM), jnp.float32))
    attended_low = attended.reshape(tokens, D).astype(jnp.bfloat16)
    residual = inputs + product(attended_low, w_out)
    second_norm, second_inverse = norm_forward(residual, norm2_gain)
    second_low = second_norm.astype(jnp.bfloat16)
    gate_values = product(second_low, w_gate)
    up_values = product(second_low, w_up)
    sigmoid_gate = jax.nn.sigmoid(gate_values)
    activated = gate_values * sigmoid_gate
    hidden_low = (activated * up_values).astype(jnp.bfloat16)
    output = (residual + product(hidden_low, w_down)).astype(jnp.bfloat16)
    upstream = output_grad[0]
    grad_down = product_tn(hidden_low, upstream)
    grad_hidden = product_nt(upstream, w_down)
    grad_gate_low = (
        grad_hidden * up_values * sigmoid_gate * (1.0 + gate_values * (1.0 - sigmoid_gate))
    ).astype(jnp.bfloat16)
    grad_up_low = (grad_hidden * activated).astype(jnp.bfloat16)
    grad_gate = product_tn(second_low, grad_gate_low)
    grad_up = product_tn(second_low, grad_up_low)
    grad_second = product_nt(grad_gate_low, w_gate) + product_nt(grad_up_low, w_up)
    grad_residual, grad_norm2 = norm_backward(residual, second_inverse, norm2_gain, grad_second)
    grad_residual = grad_residual + upstream.astype(jnp.float32)
    residual_low = grad_residual.astype(jnp.bfloat16)
    grad_out = product_tn(attended_low, residual_low)
    grad_attended = product_nt(residual_low, w_out).astype(jnp.bfloat16)
    grad_heads = grad_attended.reshape(tokens, HEADS, HEAD_DIM)

    def probs_pair(key_block, value_block, open_mask):
        probs = jnp.exp(block_scores(key_block, open_mask) - log_totals[..., None])
        dprobs = jnp.einsum(
            "qhd,khd->hqk", grad_heads, value_block, preferred_element_type=jnp.float32
        )
        return (probs, dprobs)

    def delta_step(total, block, key_block, value_block, open_mask, own):
        probs, dprobs = probs_pair(key_block, value_block, open_mask)
        return total + jnp.sum(probs * dprobs, axis=2)

    delta_rows = sweep(delta_step, jnp.zeros((HEADS, tokens), jnp.float32))

    def grad_step(carry, block, key_block, value_block, open_mask, own):
        grad_query, key_terms, value_terms = carry
        probs, dprobs = probs_pair(key_block, value_block, open_mask)
        dscores = (probs * (dprobs - delta_rows[..., None])).astype(jnp.bfloat16)
        grad_query = grad_query + jnp.einsum(
            "hqk,khd->qhd", dscores, key_block, preferred_element_type=jnp.float32
        )
        if own:
            key_part = (
                jnp.einsum("hqk,qhd->khd", dscores, query_heads, preferred_element_type=jnp.float32)
                * score_scale
            )
            value_part = jnp.einsum(
                "hqk,qhd->khd",
                probs.astype(jnp.bfloat16),
                grad_heads,
                preferred_element_type=jnp.float32,
            )
            key_terms = lax.dynamic_update_index_in_dim(key_terms, key_part, block, 0)
            value_terms = lax.dynamic_update_index_in_dim(value_terms, value_part, block, 0)
        return (grad_query, key_terms, value_terms)

    term_shape = key_blocks.shape
    start_grads = (
        jnp.zeros((tokens, HEADS, HEAD_DIM), jnp.float32),
        jnp.zeros(term_shape, jnp.float32),
        jnp.zeros(term_shape, jnp.float32),
    )
    grad_query, key_terms, value_terms = sweep(grad_step, start_grads)
    grad_queries = (grad_query * score_scale).reshape(tokens, D)
    grad_keys, grad_values = (
        lax.psum_scatter(
            key_terms.astype(jnp.bfloat16), "seq", scatter_dimension=0, tiled=True
        ).astype(jnp.float32),
        lax.psum_scatter(
            value_terms.astype(jnp.bfloat16), "seq", scatter_dimension=0, tiled=True
        ).astype(jnp.float32),
    )
    grad_projected = jnp.concatenate(
        [
            rotate(grad_queries, cosine_table, sine_table, -1.0),
            rotate(grad_keys.reshape(tokens, D), cosine_table, sine_table, -1.0),
            grad_values.reshape(tokens, D),
        ],
        axis=1,
    ).astype(jnp.bfloat16)
    grad_qkv = product_tn(first_low, grad_projected)
    grad_first = product_nt(grad_projected, w_qkv)
    grad_inputs, grad_norm1 = norm_backward(inputs, first_inverse, norm1_gain, grad_first)
    input_grad = (grad_inputs + grad_residual)[None]
    shares = (
        lax.psum_scatter(
            grad_norm1.astype(jnp.bfloat16), "seq", scatter_dimension=0, tiled=True
        ).astype(jnp.float32),
        lax.psum_scatter(
            grad_norm2.astype(jnp.bfloat16), "seq", scatter_dimension=0, tiled=True
        ).astype(jnp.float32),
        lax.psum_scatter(
            grad_qkv.astype(jnp.bfloat16), "seq", scatter_dimension=0, tiled=True
        ).astype(jnp.float32),
        lax.psum_scatter(
            grad_out.astype(jnp.bfloat16), "seq", scatter_dimension=0, tiled=True
        ).astype(jnp.float32),
        lax.psum_scatter(
            grad_gate.astype(jnp.bfloat16), "seq", scatter_dimension=0, tiled=True
        ).astype(jnp.float32),
        lax.psum_scatter(
            grad_up.astype(jnp.bfloat16), "seq", scatter_dimension=0, tiled=True
        ).astype(jnp.float32),
        lax.psum_scatter(
            grad_down.astype(jnp.bfloat16), "seq", scatter_dimension=0, tiled=True
        ).astype(jnp.float32),
    )
    totals = (
        lax.psum(shares[0].astype(jnp.bfloat16), "seg").astype(jnp.float32),
        lax.psum(shares[1].astype(jnp.bfloat16), "seg").astype(jnp.float32),
        lax.psum(shares[2].astype(jnp.bfloat16), "seg").astype(jnp.float32),
        lax.psum(shares[3].astype(jnp.bfloat16), "seg").astype(jnp.float32),
        lax.psum(shares[4].astype(jnp.bfloat16), "seg").astype(jnp.float32),
        lax.psum(shares[5].astype(jnp.bfloat16), "seg").astype(jnp.float32),
        lax.psum(shares[6].astype(jnp.bfloat16), "seg").astype(jnp.float32),
    )
    return (
        output[None],
        input_grad,
        totals[0],
        totals[1],
        totals[2],
        totals[3],
        totals[4],
        totals[5],
        totals[6],
    )


def solution(mesh):
    placed = (
        P("seg", "seq", None),
        P("seg", "seq", None),
        P(),
        P(),
        P(),
        P(),
        P(),
        P(),
        P(),
        P("seg", "seq", None),
        P("seg", "seq", None),
        P(),
        P(),
    )
    return jax.shard_map(
        on_device,
        mesh=mesh,
        in_specs=placed,
        out_specs=(
            P("seg", "seq", None),
            P("seg", "seq", None),
            P("seq"),
            P("seq"),
            P("seq", None),
            P("seq", None),
            P("seq", None),
            P("seq", None),
            P("seq", None),
        ),
        check_vma=False,
    )
```

profile of v0, /device:TPU:0, one launch (start us, length us, event | category | flops | bytes accessed | tf_op | source)
XLA Modules:
  0.0 1502.4 jit_solution(4767216906355732668)
XLA Ops:
  10.8 6.0 fusion.176
  39.9 19.3 %all-gather.7.cloned.1.call-done = bf16[8,256,1024]{2,1,0:T(8,128)(2,1)} async-done(((bf16[1,256,1024]{2,1,0:T(8,128)(2,1)}), bf16[8,256,1024]{2,1,0:T(8,128)(2,1)}) %all-gather.7.cloned.1.call-update) | async-done | bytes 4194320 | tf_op jit(solution)/shard_map/all_gather | solution.py:85
  63.4 43.1 %all-gather.11.cloned.1.call-done = bf16[8,256,1024]{2,1,0:T(8,128)(2,1)} async-done(((bf16[1,256,1024]{2,1,0:T(8,128)(2,1)}), bf16[8,256,1024]{2,1,0:T(8,128)(2,1)}) %all-gather.11.cloned.1.call-update) | async-done | bytes 4194320 | tf_op jit(solution)/shard_map/all_gather | solution.py:84
  118.4 41.9 %all-gather.15.cloned.1.call-done = bf16[2048,1024]{1,0:T(8,128)(2,1)} async-done(((bf16[512,1024]{1,0:T(8,128)(2,1)}), bf16[2048,1024]{1,0:T(8,128)(2,1)}) %all-gather.15.cloned.1.call-update) | async-done | bytes 4194320 | tf_op jit(solution)/shard_map/all_gather | solution.py:106
  166.5 48.7 %all-gather.17.cloned.1.call-done = bf16[2048,1024]{1,0:T(8,128)(2,1)} async-done(((bf16[512,1024]{1,0:T(8,128)(2,1)}), bf16[2048,1024]{1,0:T(8,128)(2,1)}) %all-gather.17.cloned.1.call-update) | async-done | bytes 4194320 | tf_op jit(solution)/shard_map/all_gather | solution.py:107
  221.9 83.1 %all-gather.13.cloned.1.call-done = bf16[4,1024,1024]{2,1,0:T(8,128)(2,1)} async-done(((bf16[4,256,1024]{2,1,0:T(8,128)(2,1)}), bf16[4,1024,1024]{2,1,0:T(8,128)(2,1)}) %all-gather.13.cloned.1.call-update) | async-done | bytes 8388624 | tf_op jit(solution)/shard_map/all_gather | solution.py:90
  305.0 8.9 copy.127
  313.9 10.1 copy.87
  324.0 88.0 %while.112 = (s32[]{:T(128)}, f32[8,512]{1,0:T(8,128)S(1)}, f32[8,512]{1,0:T(8,128)S(1)}, bf16[8,512,8,128]{3,1,2,0:T(8,128)(2,1)}, bf16[512,8,128]{2,0,1:T(8,128)(2,1)S(1)}, /*index=5*/pred[]{:T(512)}, s32[]{:T(128)}, s32[]{:T(128)}) while((s32[]{:T(128)}, f32[8,512]{1,0:T(8,128)S(1)}, f32[8,512]{1,0:T(8,128)S(1)}, ...), condition=%wide.region_4.6_spmd.clone, body=%wide.region_1.5_spmd.clone.sunk | while | flops 551571456 | bytes 19088480 | solution.py:141
  324.4 5.8 fusion.292
  335.4 5.8 fusion.292
  346.3 5.8 fusion.292
  357.3 5.8 fusion.292
  368.2 5.8 fusion.292
  379.2 5.8 fusion.292
  390.1 5.8 fusion.292
  401.1 5.8 fusion.292
  416.8 8.9 copy.126
  425.7 9.1 copy.102
  434.8 85.3 %while.113 = (s32[]{:T(128)}, f32[512,8,128]{0,2,1:T(8,128)}, bf16[8,512,8,128]{3,2,1,0:T(8,128)(2,1)}, bf16[8,512,8,128]{3,1,2,0:T(8,128)(2,1)}, bf16[512,8,128...) while((s32[]{:T(128)}, f32[512,8,128]{0,2,1:T(8,128)}, ...), condition=%wide.region_10.12_spmd.clone, body=%wide.region_9.11_spmd.clone.sunk | while | flops 1083179008 | bytes 11551851 | solution.py:141
  449.7 6.1 bitcast_add_fusion.12
  460.4 6.1 bitcast_add_fusion.12
  471.2 6.1 bitcast_add_fusion.12
  481.9 6.1 bitcast_add_fusion.12
  492.6 6.1 bitcast_add_fusion.12
  503.4 6.1 bitcast_add_fusion.12
  514.1 6.1 bitcast_add_fusion.12
  520.2 11.2 while.109
  525.1 6.3 bitcast_add_fusion.10
  545.4 11.5 multiply_convert_fusion
  556.9 6.0 fusion.184
  569.2 48.3 %while.114 = (s32[]{:T(128)}, f32[8,512]{1,0:T(8,128)S(1)}, bf16[8,512,8,128]{3,1,2,0:T(8,128)(2,1)}, bf16[512,8,128]{2,0,1:T(8,128)(2,1)S(1)}, f32[8,512]{1,0:T...) while((s32[]{:T(128)}, f32[8,512]{1,0:T(8,128)S(1)}, ...), condition=%wide.region_17.19_spmd.clone, body=%wide.region_15.18_spmd.clone.sunk | while | flops 1084231680 | bytes 21055084 | solution.py:141
  618.5 13.1 while.110
  618.9 5.9 fusion.277
  625.0 6.5 fusion.278
  631.6 106.0 %while.115 = (s32[]{:T(128)}, f32[512,8,128]{0,2,1:T(8,128)S(1)}, bf16[8,512,8,128]{3,1,2,0:T(8,128)(2,1)}, bf16[512,8,128]{2,0,1:T(8,128)(2,1)S(1)}, f32[8,512]...) while((s32[]{:T(128)}, f32[512,8,128]{0,2,1:T(8,128)S(1)}, ...), condition=%wide.region_22.24_spmd.clone, body=%wide.region_21.23_spmd.clone.sunk | while | flops 1624244224 | bytes 26249336 | solution.py:141
  631.6 5.7 fusion.310
  637.3 7.5 bitcast_add_fusion.13
  650.6 7.5 bitcast_add_fusion.13
  663.8 7.5 bitcast_add_fusion.13
  677.1 7.5 bitcast_add_fusion.13
  690.3 7.5 bitcast_add_fusion.13
  703.6 7.5 bitcast_add_fusion.13
  716.8 7.5 bitcast_add_fusion.13
  730.1 7.5 bitcast_add_fusion.13
  743.4 22.3 %while.111 = (s32[]{:T(128)}, f32[512,8,128]{0,2,1:T(8,128)S(1)}, bf16[4,512,8,128]{3,1,2,0:T(8,128)(2,1)}, bf16[4,512,8,128]{3,1,2,0:T(8,128)(2,1)}, s32[]{:T(1...) while((s32[]{:T(128)}, f32[512,8,128]{0,2,1:T(8,128)S(1)}, ...), condition=%wide.region_24.26_spmd.clone, body=%wide.region_23.25_spmd.clone.sunk | while | flops 2706637824 | bytes 117236072 | solution.py:142
  743.6 5.8 fusion.289
  749.6 6.7 fusion.290
  771.5 7.8 convolution_convert_fusion.1
  780.6 6.8 convolution_convert_fusion.2
  788.6 6.9 convolution_convert_fusion
  802.1 168.8 %reduce-scatter.22.cloned.1.call-done = bf16[1,512,8,128]{3,1,2,0:T(8,128)(2,1)} async-done(((bf16[4,512,8,128]{3,1,2,0:T(8,128)(2,1)}), bf16[1,512,8,128]{3,1,2,0:T(8,128)(2,1)}) %reduce-scatter.22.cloned.1.call-update) | async-done | bytes 1048592
  978.9 47.6 %reduce-scatter.24.cloned.1.call-done = bf16[1,512,8,128]{3,1,2,0:T(8,128)(2,1)} async-done(((bf16[4,512,8,128]{3,1,2,0:T(8,128)(2,1)}), bf16[1,512,8,128]{3,1,2,0:T(8,128)(2,1)}) %reduce-scatter.24.cloned.1.call-update) | async-done | bytes 1048592
  1033.2 5.9 convolution_convert_fusion.3
  1039.4 25.3 %reduce-scatter.14.cloned.1.call-done = bf16[256,1024]{1,0:T(8,128)(2,1)} async-done(((bf16[1024,1024]{1,0:T(8,128)(2,1)}), bf16[256,1024]{1,0:T(8,128)(2,1)}) %reduce-scatter.14.cloned.1.call-update) | async-done | bytes 524304 | tf_op jit(solution)/shard_map/reduce_scatter | solution.py:266
  1064.7 68.5 %reduce-scatter.18.cloned.1.call-done = bf16[256,2816]{1,0:T(8,128)(2,1)} async-done(((bf16[1024,2816]{1,0:T(8,128)(2,1)}), bf16[256,2816]{1,0:T(8,128)(2,1)}) %reduce-scatter.18.cloned.1.call-update) | async-done | bytes 1441808 | tf_op jit(solution)/shard_map/reduce_scatter | solution.py:272
  1133.2 68.7 %reduce-scatter.16.cloned.1.call-done = bf16[256,2816]{1,0:T(8,128)(2,1)} async-done(((bf16[1024,2816]{1,0:T(8,128)(2,1)}), bf16[256,2816]{1,0:T(8,128)(2,1)}) %reduce-scatter.16.cloned.1.call-update) | async-done | bytes 1441808 | tf_op jit(solution)/shard_map/reduce_scatter | solution.py:269
  1201.9 68.5 %reduce-scatter.20.cloned.1.call-done = bf16[704,1024]{1,0:T(8,128)(2,1)} async-done(((bf16[2816,1024]{1,0:T(8,128)(2,1)}), bf16[704,1024]{1,0:T(8,128)(2,1)}) %reduce-scatter.20.cloned.1.call-update) | async-done | bytes 1441808 | tf_op jit(solution)/shard_map/reduce_scatter | solution.py:275
  1270.5 73.0 %reduce-scatter.12.cloned.1.call-done = bf16[256,3072]{1,0:T(8,128)(2,1)} async-done(((bf16[1024,3072]{1,0:T(8,128)(2,1)}), bf16[256,3072]{1,0:T(8,128)(2,1)}) %reduce-scatter.12.cloned.1.call-update) | async-done | bytes 1572880 | tf_op jit(solution)/shard_map/reduce_scatter | solution.py:263
  1345.5 7.8 fusion.166
  1353.3 8.1 fusion.157
  1361.4 8.9 all-reduce.6
  1370.4 15.4 %all-reduce.4 = (bf16[256]{0:T(256)(128)(2,1)S(1)}, bf16[256]{0:T(256)(128)(2,1)S(1)}) all-reduce(bf16[256]{0:T(256)(128)(2,1)S(1)} %dynamic-slice.5, bf16[256]{0:T(256)(128)(2,1)S(1)} %dynamic-slice.7), channel_id=1, replica_groups=mesh['seg'=8,'seq'=4] {'seg'}, use_global_device_ids=true, to_apply=%region_30.32 | all-reduce | flops 512 | bytes 2048 | tf_op jit(solution)/shard_map/psum | solution.py:280
  1390.5 94.6 %all-reduce.9.cloned.1.call-done = (bf16[256,3072]{1,0:T(8,128)(2,1)}, bf16[256,1024]{1,0:T(8,128)(2,1)}, bf16[256,2816]{1,0:T(8,128)(2,1)}, bf16[256,2816]{1,0:T(8,128)(2,1)}, bf16[704,1024]{1,0:T(8,128)(2,1)}) async-done(((bf16[256,3072]{1,0:T(8,128)(2,1)}, bf16[256,1024]{1,0:T(8,128)(2,1)}, bf16[256,2816]{1,0:T(8,128)(2,1)}, bf16[256,2816]{1,0:T(8,128)(2,1)}, bf16[704,1024]{1,0:T(8,128)(2,1)}), ...) | async-done | bytes 6422544 | tf_op jit(solution)/shard_map/psum | solution.py:282
  (320 shorter events, 323.4 us)
Async XLA Ops:
  7.2 526.1 %copy-start = (bf16[1024,1024]{1,0:T(8,128)(2,1)S(1)}, bf16[1024,1024]{1,0:T(8,128)(2,1)}, u32[]{:S(2)}) copy-start(bf16[1024,1024]{1,0:T(8,128)(2,1)} %param.36) | copy-start | bytes 6291460
  7.2 52.0 %all-gather.7.cloned.1.call-start = ((), (), s32[]{:S(2)}) async-start(), calls=%async_computation.7 | async-start | bytes 4718592 | tf_op jit(solution)/shard_map/all_gather | solution.py:85
  7.9 98.6 %all-gather.11.cloned.1.call-start = ((), (), s32[]{:S(2)}) async-start(), calls=%async_computation.9 | async-start | bytes 4718592 | tf_op jit(solution)/shard_map/all_gather | solution.py:84
  8.7 151.7 %all-gather.15.cloned.1.call-start = ((), (), s32[]{:S(2)}) async-start(), calls=%async_computation.11 | async-start | bytes 5242880 | tf_op jit(solution)/shard_map/all_gather | solution.py:106
  10.8 6.0 copy-start.43
  16.8 2.6 copy-start.11
  29.9 2.2 slice-start.2
  30.0 3.7 slice-start.3
  31.3 5.4 copy-start.7
  36.7 2.9 copy-start.46
  36.7 178.5 %all-gather.17.cloned.1.call-start = ((), (), s32[]{:S(2)}) async-start(), calls=%async_computation.12 | async-start | bytes 5242880 | tf_op jit(solution)/shard_map/all_gather | solution.py:107
  39.6 265.4 %all-gather.13.cloned.1.call-start = ((), (), s32[]{:S(2)}) async-start(), calls=%async_computation.10 | async-start | bytes 10485760 | tf_op jit(solution)/shard_map/all_gather | solution.py:90
  115.4 1.8 copy-start.48
  115.4 301.4 %all-gather.9.cloned.1.call-start = ((), (), s32[]{:S(2)}) async-start(), calls=%async_computation.8 | async-start | bytes 10485760 | tf_op jit(solution)/shard_map/all_gather | solution.py:91
  218.5 3.3 copy-start.3
  221.8 749.1 %reduce-scatter.22.cloned.1.call-start = ((), (), s32[]{:S(2)}) async-start(), calls=%async_computation.18 | async-start | bytes 5242880
  531.3 1.9 copy-start.12
  531.3 3.6 slice-start.4
  533.3 2.2 slice-start.5
  533.3 7.2 slice-start.6
  534.7 32.3 %copy-start.4 = (f32[512,1024]{1,0:T(8,128)}, f32[512,1024]{1,0:T(8,128)S(1)}, u32[]{:S(2)}) copy-start(f32[512,1024]{1,0:T(8,128)S(1)} %get-tuple-element.1348) | copy-start | bytes 6291460
  535.5 5.0 copy-start.32
  535.5 5.0 slice-start.7
  540.5 5.0 copy-start.28
  556.9 6.0 copy-start.50
  567.6 1.5 copy-start.22
  618.5 13.1 copy-start.2
  749.6 6.7 copy-start.9
  756.3 6.3 slice-start
  757.9 2.0 copy-start.10
  759.9 2.7 slice-start.1
  759.9 2.8 copy-start.35
  765.8 260.7 %reduce-scatter.24.cloned.1.call-start = ((), (), s32[]{:S(2)}) async-start(), calls=%async_computation.19 | async-start | bytes 5242880
  766.5 298.2 %reduce-scatter.14.cloned.1.call-start = ((), (), s32[]{:S(2)}) async-start(), calls=%async_computation.14 | async-start | bytes 2621440 | tf_op jit(solution)/shard_map/reduce_scatter | solution.py:266
  771.2 362.0 %reduce-scatter.18.cloned.1.call-start = ((), (), s32[]{:S(2)}) async-start(), calls=%async_computation.16 | async-start | bytes 7208960 | tf_op jit(solution)/shard_map/reduce_scatter | solution.py:272
  779.4 422.6 %reduce-scatter.16.cloned.1.call-start = ((), (), s32[]{:S(2)}) async-start(), calls=%async_computation.15 | async-start | bytes 7208960 | tf_op jit(solution)/shard_map/reduce_scatter | solution.py:269
  787.4 483.1 %reduce-scatter.20.cloned.1.call-start = ((), (), s32[]{:S(2)}) async-start(), calls=%async_computation.17 | async-start | bytes 7208960 | tf_op jit(solution)/shard_map/reduce_scatter | solution.py:275
  795.5 548.1 %reduce-scatter.12.cloned.1.call-start = ((), (), s32[]{:S(2)}) async-start(), calls=%async_computation.13 | async-start | bytes 7864320 | tf_op jit(solution)/shard_map/reduce_scatter | solution.py:263
  972.2 1.6 copy-start.6
  972.3 2.2 copy-start.17
  972.3 2.8 copy-start.18
  972.3 2.8 copy-start.26
  972.3 2.8 copy-start.27
  977.6 51.1 %copy-start.19 = (bf16[1,512,8,128]{3,1,2,0:T(8,128)(2,1)S(1)}, bf16[1,512,8,128]{3,1,2,0:T(8,128)(2,1)}, u32[]{:S(2)}) copy-start(bf16[1,512,8,128]{3,1,2,0:T(8,128)(2,1)} %reduce-scatter.22.cloned.1.call-done) | copy-start | bytes 3145732
  1028.4 2.0 copy-start.8
  1028.4 2.6 copy-start.16
  1028.7 3.5 copy-start.38
  1031.0 2.2 copy-start.13
  1031.0 2.2 copy-start.36
  1031.0 2.2 copy-start.44
  1031.0 2.2 copy-start.45
  1039.1 446.0 %all-reduce.9.cloned.1.call-start = ((), (), s32[]{:S(2)}) async-start(), calls=%async_computation.20 | async-start | bytes 12845056 | tf_op jit(solution)/shard_map/psum | solution.py:282
  1343.5 1.9 copy-start.5
  1345.4 7.8 copy-start.31
  1345.4 7.8 copy-start.37
  1345.5 7.8 copy-start.39
  1353.2 8.1 copy-start.47
  1353.3 33.7 %copy-start.15 = (f32[512,1024]{1,0:T(8,128)S(1)}, f32[512,1024]{1,0:T(8,128)}, u32[]{:S(2)}) copy-start(f32[512,1024]{1,0:T(8,128)} %copy-done.14) | copy-start | bytes 6291460
  1353.3 33.7 %copy-start.42 = (f32[512]{0:T(512)S(1)}, f32[512]{0:T(512)}, u32[]{:S(2)}) copy-start(f32[512]{0:T(512)} %get-tuple-element.1341) | copy-start | bytes 6148
  1485.1 3.6 copy-start.25
  1488.6 1.9 copy-start.24
  1490.4 1.9 copy-start.23
  1492.3 1.9 copy-start.40
  1492.3 3.0 copy-start.1
  (9 other events, 10.6 us)
Sparse Core Ops, SparseCore 0:
  9.6 49.5 all-gather.6
  60.8 45.6 all-gather.10
  109.0 51.3 all-gather.14
  162.6 52.5 all-gather.16
  217.5 87.4 all-gather.12
  307.3 87.4 all-gather.8
  765.9 204.9 reduce-scatter.21
  973.8 52.5 reduce-scatter.23
  1029.5 35.1 reduce-scatter.13
  1067.5 65.6 reduce-scatter.17
  1136.2 65.6 reduce-scatter.15
  1204.8 65.6 reduce-scatter.19
  1273.5 70.0 reduce-scatter.11
  1346.1 138.8 all-reduce.8
where the time goes:
time: 1510 us; the launch traced here: 1500 us
  waiting for transfers between devices  854 us (57%)
  matrix products  377 us (25%)
  local copies, waits for them, and re-layouts  138 us (9%)
  other arithmetic  89.1 us (6%)
  blocking collectives  24.3 us (2%)
  between operations  16.4 us (1%)
    unnamed x16, waiting for transfers between devices  219 us
    dot_general x27, matrix products, block_scores(): jnp.einsum('qhd,khd->hqk', query_heads, key_block, preferred_element_type...  127 us
    psum x1, waiting for transfers between devices, on_device(): lax.psum(shares[2].astype(jnp.bfloat16), 'seg').astype(jnp.float32)  94.6 us
    all_gather x1, waiting for transfers between devices, on_device(): lax.all_gather(chosen_keys, 'seq', axis=1, tiled=True)  83.1 us
    reduce_scatter x1, waiting for transfers between devices, on_device(): lax.psum_scatter(grad_qkv.astype(jnp.bfloat16), 'seq', scatter_dimension=...  73 us
    unnamed x123, local copies, waits for them, and re-layouts  69.1 us
    reduce_scatter x1, waiting for transfers between devices, on_device(): lax.psum_scatter(grad_gate.astype(jnp.bfloat16), 'seq', scatter_dimension...  68.7 us
    reduce_scatter x1, waiting for transfers between devices, on_device(): lax.psum_scatter(grad_down.astype(jnp.bfloat16), 'seq', scatter_dimension...  68.5 us
  transfers between devices with their start and end apart: 14, of which 13 were waited for; matrix products, arithmetic and copies ran while one was open for 16% of the time, Pallas kernels for 0%

commit v1 on v0

--- a/solution.py
+++ b/solution.py
@@ -279,7 +279,7 @@
     totals = (
         lax.psum(shares[0].astype(jnp.bfloat16), "seg").astype(jnp.float32),
         lax.psum(shares[1].astype(jnp.bfloat16), "seg").astype(jnp.float32),
-        lax.psum(shares[2].astype(jnp.bfloat16), "seg").astype(jnp.float32),
+        jnp.sum(lax.all_gather(shares[2].astype(jnp.bfloat16), "seg"), axis=0).astype(jnp.float32),
         lax.psum(shares[3].astype(jnp.bfloat16), "seg").astype(jnp.float32),
         lax.psum(shares[4].astype(jnp.bfloat16), "seg").astype(jnp.float32),
         lax.psum(shares[5].astype(jnp.bfloat16), "seg").astype(jnp.float32),

time: 1510 us -> 1680 us (1.11)
  waiting for transfers between devices: 854 us -> 1010 us
    all_gather x0 -> x1, waiting for transfers between devices: none -> 109 us  [on_device(): lax.all_gather(shares[2].astype(jnp.bfloat16), 'seg')]
    all_gather x1, waiting for transfers between devices: 0.02 us -> 81.6 us  [on_device(): lax.all_gather(chosen_values, 'seq', axis=1, tiled=True)]
    psum x1, waiting for transfers between devices: 94.6 us -> 65.4 us  [on_device(): lax.psum(shares[3].astype(jnp.bfloat16), 'seg').astype(jnp.float32)]
    all_gather x1, waiting for transfers between devices: 43.1 us -> 18.8 us  [on_device(): lax.all_gather(mem_keys, 'seg', axis=0, tiled=True)]
    all_gather x1, waiting for transfers between devices: 19.3 us -> 43.1 us  [on_device(): lax.all_gather(mem_values, 'seg', axis=0, tiled=True)]
    unnamed x16 -> x17, waiting for transfers between devices: 219 us -> 224 us
    unnamed x123 -> x117, local copies, waits for them, and re-layouts: 69.1 us -> 69.9 us
  transfers between devices with their start and end apart: 14 -> 15, of which waited for: 13 -> 15; matrix products, arithmetic and copies ran while one was open for 16% -> 8% of each run, Pallas kernels for 0% -> 0%
where the time goes in v1:
time: 1680 us; the launch traced here: 1670 us
  waiting for transfers between devices  1010 us (60%)
  matrix products  376 us (22%)
  local copies, waits for them, and re-layouts  139 us (8%)
  other arithmetic  98.7 us (6%)
  blocking collectives  24.4 us (1%)
    unnamed x17, waiting for transfers between devices  224 us
    dot_general x27, matrix products, block_scores(): jnp.einsum('qhd,khd->hqk', query_heads, key_block, preferred_element_type...  127 us
    all_gather x1, waiting for transfers between devices, on_device(): lax.all_gather(shares[2].astype(jnp.bfloat16), 'seg')  109 us
    all_gather x1, waiting for transfers between devices, on_device(): lax.all_gather(chosen_values, 'seq', axis=1, tiled=True)  81.6 us
    all_gather x1, waiting for transfers between devices, on_device(): lax.all_gather(chosen_keys, 'seq', axis=1, tiled=True)  80.9 us
    reduce_scatter x1, waiting for transfers between devices, on_device(): lax.psum_scatter(grad_qkv.astype(jnp.bfloat16), 'seq', scatter_dimension=...  72.7 us
    unnamed x117, local copies, waits for them, and re-layouts  69.9 us
    reduce_scatter x1, waiting for transfers between devices, on_device(): lax.psum_scatter(grad_up.astype(jnp.bfloat16), 'seq', scatter_dimension=0...  68.7 us
  transfers between devices with their start and end apart: 15, of which 15 were waited for; matrix products, arithmetic and copies ran while one was open for 8% of the time, Pallas kernels for 0%

profile of v1, /device:TPU:0, one launch (start us, length us, event | category | flops | bytes accessed | tf_op | source)
XLA Modules:
  0.0 1672.4 jit_solution(14979190047099461669)
XLA Ops:
  11.4 6.0 fusion.176
  40.4 18.8 %all-gather.13.cloned.1.call-done = bf16[8,256,1024]{2,1,0:T(8,128)(2,1)} async-done(((bf16[1,256,1024]{2,1,0:T(8,128)(2,1)}), bf16[8,256,1024]{2,1,0:T(8,128)(2,1)}) %all-gather.13.cloned.1.call-update) | async-done | bytes 4194320 | tf_op jit(solution)/shard_map/all_gather | solution.py:84
  63.4 43.1 %all-gather.9.cloned.1.call-done = bf16[8,256,1024]{2,1,0:T(8,128)(2,1)} async-done(((bf16[1,256,1024]{2,1,0:T(8,128)(2,1)}), bf16[8,256,1024]{2,1,0:T(8,128)(2,1)}) %all-gather.9.cloned.1.call-update) | async-done | bytes 4194320 | tf_op jit(solution)/shard_map/all_gather | solution.py:85
  119.2 41.2 %all-gather.17.cloned.1.call-done = bf16[2048,1024]{1,0:T(8,128)(2,1)} async-done(((bf16[512,1024]{1,0:T(8,128)(2,1)}), bf16[2048,1024]{1,0:T(8,128)(2,1)}) %all-gather.17.cloned.1.call-update) | async-done | bytes 4194320 | tf_op jit(solution)/shard_map/all_gather | solution.py:106
  166.5 48.7 %all-gather.19.cloned.1.call-done = bf16[2048,1024]{1,0:T(8,128)(2,1)} async-done(((bf16[512,1024]{1,0:T(8,128)(2,1)}), bf16[2048,1024]{1,0:T(8,128)(2,1)}) %all-gather.19.cloned.1.call-update) | async-done | bytes 4194320 | tf_op jit(solution)/shard_map/all_gather | solution.py:107
  223.4 81.6 %all-gather.11.cloned.1.call-done = bf16[4,1024,1024]{2,1,0:T(8,128)(2,1)} async-done(((bf16[4,256,1024]{2,1,0:T(8,128)(2,1)}), bf16[4,1024,1024]{2,1,0:T(8,128)(2,1)}) %all-gather.11.cloned.1.call-update) | async-done | bytes 8388624 | tf_op jit(solution)/shard_map/all_gather | solution.py:91
  305.0 8.9 copy.126
  313.9 80.9 %all-gather.15.cloned.1.call-done = bf16[4,1024,1024]{2,1,0:T(8,128)(2,1)} async-done(((bf16[4,256,1024]{2,1,0:T(8,128)(2,1)}), bf16[4,1024,1024]{2,1,0:T(8,128)(2,1)}) %all-gather.15.cloned.1.call-update) | async-done | bytes 8388624 | tf_op jit(solution)/shard_map/all_gather | solution.py:90
  394.8 8.9 copy.127
  403.7 9.0 copy.87
  412.7 87.6 %while.112 = (s32[]{:T(128)}, f32[8,512]{1,0:T(8,128)S(1)}, f32[8,512]{1,0:T(8,128)S(1)}, bf16[8,512,8,128]{3,1,2,0:T(8,128)(2,1)}, bf16[512,8,128]{2,0,1:T(8,128)(2,1)S(1)}, /*index=5*/pred[]{:T(512)}, s32[]{:T(128)}, s32[]{:T(128)}) while((s32[]{:T(128)}, f32[8,512]{1,0:T(8,128)S(1)}, f32[8,512]{1,0:T(8,128)S(1)}, ...), condition=%wide.region_4.6_spmd.clone, body=%wide.region_1.5_spmd.clone.sunk | while | flops 551571456 | bytes 19087980 | solution.py:141
  413.1 5.8 fusion.292
  424.0 5.8 fusion.292
  434.9 5.8 fusion.292
  445.8 5.8 fusion.292
  456.7 5.8 fusion.292
  467.6 5.8 fusion.292
  478.5 5.8 fusion.292
  489.4 5.8 fusion.292
  505.0 9.0 copy.102
  514.1 85.2 %while.113 = (s32[]{:T(128)}, f32[512,8,128]{0,2,1:T(8,128)}, bf16[8,512,8,128]{3,2,1,0:T(8,128)(2,1)}, bf16[8,512,8,128]{3,1,2,0:T(8,128)(2,1)}, bf16[512,8,128...) while((s32[]{:T(128)}, f32[512,8,128]{0,2,1:T(8,128)}, ...), condition=%wide.region_10.12_spmd.clone, body=%wide.region_9.11_spmd.clone.sunk | while | flops 1083179008 | bytes 11551351 | solution.py:141
  528.8 6.1 bitcast_add_fusion.12
  539.5 6.1 bitcast_add_fusion.12
  550.3 6.1 bitcast_add_fusion.12
  561.0 6.1 bitcast_add_fusion.12
  571.7 6.1 bitcast_add_fusion.12
  582.5 6.1 bitcast_add_fusion.12
  593.2 6.1 bitcast_add_fusion.12
  599.3 11.3 while.109
  604.3 6.3 bitcast_add_fusion.10
  624.8 11.9 multiply_convert_fusion
  648.1 48.3 %while.114 = (s32[]{:T(128)}, f32[8,512]{1,0:T(8,128)S(1)}, bf16[8,512,8,128]{3,1,2,0:T(8,128)(2,1)}, bf16[512,8,128]{2,0,1:T(8,128)(2,1)S(1)}, f32[8,512]{1,0:T...) while((s32[]{:T(128)}, f32[8,512]{1,0:T(8,128)S(1)}, ...), condition=%wide.region_17.19_spmd.clone, body=%wide.region_15.18_spmd.clone.sunk | while | flops 1084231680 | bytes 21054076 | solution.py:141
  697.3 13.1 while.110
  697.7 5.9 fusion.277
  703.9 6.5 fusion.278
  710.4 106.0 %while.115 = (s32[]{:T(128)}, f32[512,8,128]{0,2,1:T(8,128)S(1)}, bf16[8,512,8,128]{3,1,2,0:T(8,128)(2,1)}, bf16[512,8,128]{2,0,1:T(8,128)(2,1)S(1)}, f32[8,512]...) while((s32[]{:T(128)}, f32[512,8,128]{0,2,1:T(8,128)S(1)}, ...), condition=%wide.region_22.24_spmd.clone, body=%wide.region_21.23_spmd.clone.sunk | while | flops 1624244224 | bytes 26249344 | solution.py:141
  716.2 7.5 bitcast_add_fusion.13
  729.4 7.5 bitcast_add_fusion.13
  742.6 7.5 bitcast_add_fusion.13
  755.9 7.5 bitcast_add_fusion.13
  769.1 7.5 bitcast_add_fusion.13
  782.4 7.5 bitcast_add_fusion.13
  795.6 7.5 bitcast_add_fusion.13
  808.9 7.5 bitcast_add_fusion.13
  822.2 22.7 %while.111 = (s32[]{:T(128)}, f32[512,8,128]{0,2,1:T(8,128)S(1)}, bf16[4,512,8,128]{3,1,2,0:T(8,128)(2,1)}, bf16[4,512,8,128]{3,1,2,0:T(8,128)(2,1)}, s32[]{:T(1...) while((s32[]{:T(128)}, f32[512,8,128]{0,2,1:T(8,128)S(1)}, ...), condition=%wide.region_24.26_spmd.clone, body=%wide.region_23.25_spmd.clone.sunk | while | flops 2706637824 | bytes 150790576 | solution.py:142
  828.4 6.7 fusion.290
  850.6 7.8 convolution_convert_fusion.2
  859.7 6.8 convolution_convert_fusion.1
  867.7 6.9 convolution_convert_fusion
  881.2 169.2 %reduce-scatter.24.cloned.1.call-done = bf16[1,512,8,128]{3,1,2,0:T(8,128)(2,1)} async-done(((bf16[4,512,8,128]{3,1,2,0:T(8,128)(2,1)}), bf16[1,512,8,128]{3,1,2,0:T(8,128)(2,1)}) %reduce-scatter.24.cloned.1.call-update) | async-done | bytes 1048592
  1053.6 52.4 %reduce-scatter.22.cloned.1.call-done = bf16[1,512,8,128]{3,1,2,0:T(8,128)(2,1)} async-done(((bf16[4,512,8,128]{3,1,2,0:T(8,128)(2,1)}), bf16[1,512,8,128]{3,1,2,0:T(8,128)(2,1)}) %reduce-scatter.22.cloned.1.call-update) | async-done | bytes 1048592
  1115.6 5.9 convolution_convert_fusion.3
  1121.6 22.7 %reduce-scatter.14.cloned.1.call-done = bf16[256,1024]{1,0:T(8,128)(2,1)} async-done(((bf16[1024,1024]{1,0:T(8,128)(2,1)}), bf16[256,1024]{1,0:T(8,128)(2,1)}) %reduce-scatter.14.cloned.1.call-update) | async-done | bytes 524304 | tf_op jit(solution)/shard_map/reduce_scatter | solution.py:266
  1144.2 68.5 %reduce-scatter.16.cloned.1.call-done = bf16[256,2816]{1,0:T(8,128)(2,1)} async-done(((bf16[1024,2816]{1,0:T(8,128)(2,1)}), bf16[256,2816]{1,0:T(8,128)(2,1)}) %reduce-scatter.16.cloned.1.call-update) | async-done | bytes 1441808 | tf_op jit(solution)/shard_map/reduce_scatter | solution.py:269
  1212.8 68.7 %reduce-scatter.18.cloned.1.call-done = bf16[256,2816]{1,0:T(8,128)(2,1)} async-done(((bf16[1024,2816]{1,0:T(8,128)(2,1)}), bf16[256,2816]{1,0:T(8,128)(2,1)}) %reduce-scatter.18.cloned.1.call-update) | async-done | bytes 1441808 | tf_op jit(solution)/shard_map/reduce_scatter | solution.py:272
  1281.5 68.5 %reduce-scatter.20.cloned.1.call-done = bf16[704,1024]{1,0:T(8,128)(2,1)} async-done(((bf16[2816,1024]{1,0:T(8,128)(2,1)}), bf16[704,1024]{1,0:T(8,128)(2,1)}) %reduce-scatter.20.cloned.1.call-update) | async-done | bytes 1441808 | tf_op jit(solution)/shard_map/reduce_scatter | solution.py:275
  1350.4 72.7 %reduce-scatter.12.cloned.1.call-done = bf16[256,3072]{1,0:T(8,128)(2,1)} async-done(((bf16[1024,3072]{1,0:T(8,128)(2,1)}), bf16[256,3072]{1,0:T(8,128)(2,1)}) %reduce-scatter.12.cloned.1.call-update) | async-done | bytes 1572880 | tf_op jit(solution)/shard_map/reduce_scatter | solution.py:263
  1424.4 7.8 fusion.166
  1432.2 8.1 fusion.157
  1440.3 8.9 all-reduce.6
  1449.4 15.4 all-reduce.4
  1469.4 65.4 %all-reduce.9.cloned.1.call-done = (bf16[256,1024]{1,0:T(8,128)(2,1)}, bf16[256,2816]{1,0:T(8,128)(2,1)}, bf16[256,2816]{1,0:T(8,128)(2,1)}, bf16[704,1024]{1,0:T(8,128)(2,1)}) async-done(((bf16[256,1024]{1,0:T(8,128)(2,1)}, bf16[256,2816]{1,0:T(8,128)(2,1)}, bf16[256,2816]{1,0:T(8,128)(2,1)}, bf16[704,1024]{1,0:T(8,128)(2,1)}), (bf16[256,1024]{1,0:T(8,128)(2,1)}, bf16[256,2816]{1,0:T(8,128)(2,1)}, ...) | async-done | bytes 4849680 | tf_op jit(solution)/shard_map/psum | solution.py:283
  1544.0 109.1 %all-gather.21.cloned.1.call-done = bf16[2048,3072]{1,0:T(8,128)(2,1)} async-done(((bf16[256,3072]{1,0:T(8,128)(2,1)}), bf16[2048,3072]{1,0:T(8,128)(2,1)}) %all-gather.21.cloned.1.call-update) | async-done | bytes 12582928 | tf_op jit(solution)/shard_map/all_gather | solution.py:282
  1653.1 8.9 reduce_sum.116
  (322 shorter events, 342.8 us)
Async XLA Ops:
  7.2 605.3 %copy-start = (bf16[1024,1024]{1,0:T(8,128)(2,1)S(1)}, bf16[1024,1024]{1,0:T(8,128)(2,1)}, u32[]{:S(2)}) copy-start(bf16[1024,1024]{1,0:T(8,128)(2,1)} %param.36) | copy-start | bytes 6291460
  7.2 52.0 %all-gather.13.cloned.1.call-start = ((), (), s32[]{:S(2)}) async-start(), calls=%async_computation.9 | async-start | bytes 4718592 | tf_op jit(solution)/shard_map/all_gather | solution.py:84
  7.9 98.6 %all-gather.9.cloned.1.call-start = ((), (), s32[]{:S(2)}) async-start(), calls=%async_computation.7 | async-start | bytes 4718592 | tf_op jit(solution)/shard_map/all_gather | solution.py:85
  8.7 151.7 %all-gather.17.cloned.1.call-start = ((), (), s32[]{:S(2)}) async-start(), calls=%async_computation.11 | async-start | bytes 5242880 | tf_op jit(solution)/shard_map/all_gather | solution.py:106
  17.4 2.6 copy-start.13
  30.5 2.3 slice-start.2
  30.5 3.7 slice-start.3
  31.8 5.4 copy-start.7
  37.3 2.9 copy-start.45
  37.3 178.0 %all-gather.19.cloned.1.call-start = ((), (), s32[]{:S(2)}) async-start(), calls=%async_computation.12 | async-start | bytes 5242880 | tf_op jit(solution)/shard_map/all_gather | solution.py:107
  40.1 264.9 %all-gather.11.cloned.1.call-start = ((), (), s32[]{:S(2)}) async-start(), calls=%async_computation.8 | async-start | bytes 10485760 | tf_op jit(solution)/shard_map/all_gather | solution.py:91
  115.4 2.5 copy-start.47
  115.4 279.4 %all-gather.15.cloned.1.call-start = ((), (), s32[]{:S(2)}) async-start(), calls=%async_computation.10 | async-start | bytes 10485760 | tf_op jit(solution)/shard_map/all_gather | solution.py:90
  116.0 934.4 %reduce-scatter.24.cloned.1.call-start = ((), (), s32[]{:S(2)}) async-start(), calls=%async_computation.20 | async-start | bytes 5242880
  218.5 2.0 copy-start.3
  610.6 1.9 copy-start.14
  610.6 3.6 slice-start.4
  612.5 2.2 slice-start.5
  612.5 7.2 slice-start.6
  613.9 32.0 %copy-start.4 = (f32[512,1024]{1,0:T(8,128)}, f32[512,1024]{1,0:T(8,128)S(1)}, u32[]{:S(2)}) copy-start(f32[512,1024]{1,0:T(8,128)S(1)} %get-tuple-element.1347) | copy-start | bytes 6291460
  614.7 5.0 copy-start.32
  614.7 5.0 slice-start.7
  619.8 5.0 copy-start.28
  636.7 5.1 copy-start.49
  646.5 1.5 copy-start.23
  697.3 13.1 copy-start.2
  828.4 11.1 slice-start
  835.1 2.7 copy-start.9
  835.1 4.4 slice-start.1
  837.8 2.5 copy-start.11
  837.8 2.7 copy-start.35
  839.4 3.4 copy-start.10
  842.9 2.0 copy-start.12
  844.9 261.1 %reduce-scatter.22.cloned.1.call-start = ((), (), s32[]{:S(2)}) async-start(), calls=%async_computation.19 | async-start | bytes 5242880
  845.7 298.6 %reduce-scatter.14.cloned.1.call-start = ((), (), s32[]{:S(2)}) async-start(), calls=%async_computation.14 | async-start | bytes 2621440 | tf_op jit(solution)/shard_map/reduce_scatter | solution.py:266
  850.4 362.4 %reduce-scatter.16.cloned.1.call-start = ((), (), s32[]{:S(2)}) async-start(), calls=%async_computation.15 | async-start | bytes 7208960 | tf_op jit(solution)/shard_map/reduce_scatter | solution.py:269
  858.5 422.9 %reduce-scatter.18.cloned.1.call-start = ((), (), s32[]{:S(2)}) async-start(), calls=%async_computation.16 | async-start | bytes 7208960 | tf_op jit(solution)/shard_map/reduce_scatter | solution.py:272
  866.5 483.5 %reduce-scatter.20.cloned.1.call-start = ((), (), s32[]{:S(2)}) async-start(), calls=%async_computation.17 | async-start | bytes 7208960 | tf_op jit(solution)/shard_map/reduce_scatter | solution.py:275
  874.6 548.4 %reduce-scatter.12.cloned.1.call-start = ((), (), s32[]{:S(2)}) async-start(), calls=%async_computation.13 | async-start | bytes 7864320 | tf_op jit(solution)/shard_map/reduce_scatter | solution.py:263
  1107.4 1.6 copy-start.6
  1107.4 2.2 copy-start.18
  1107.4 2.8 copy-start.19
  1107.4 2.8 copy-start.26
  1107.4 2.8 copy-start.27
  1110.3 1.5 copy-start.20
  1111.5 2.0 copy-start.8
  1111.8 2.9 copy-start.38
  1113.4 2.2 copy-start.15
  1113.4 2.2 copy-start.36
  1113.4 2.2 copy-start.43
  1113.4 2.2 copy-start.44
  1121.5 413.3 %all-reduce.9.cloned.1.call-start = ((), (), s32[]{:S(2)}) async-start(), calls=%async_computation.21 | async-start | bytes 9699328 | tf_op jit(solution)/shard_map/psum | solution.py:283
  1350.0 73.1 %copy-start.48 = (u32[32]{0:T(128)S(1)}, u32[32]{0:T(128)}, u32[]{:S(2)}) copy-start(u32[32]{0:T(128)} %constant.287) | copy-start | bytes 388
  1350.0 74.3 %copy-start.5 = (f32[512,1024]{1,0:T(8,128)S(1)}, f32[512,1024]{1,0:T(8,128)}, u32[]{:S(2)}) copy-start(f32[512,1024]{1,0:T(8,128)} %copy-done.4) | copy-start | bytes 6291460
  1350.0 303.1 %all-gather.21.cloned.1.call-start = ((), (), s32[]{:S(2)}) async-start(), calls=%async_computation.18 | async-start | bytes 14155776 | tf_op jit(solution)/shard_map/all_gather | solution.py:282
  1424.3 7.8 copy-start.31
  1424.4 7.8 copy-start.37
  1424.4 7.8 copy-start.39
  1432.2 8.1 copy-start.46
  1432.2 33.8 %copy-start.17 = (f32[512,1024]{1,0:T(8,128)S(1)}, f32[512,1024]{1,0:T(8,128)}, u32[]{:S(2)}) copy-start(f32[512,1024]{1,0:T(8,128)} %copy-done.16) | copy-start | bytes 6291460
  1432.2 33.8 %copy-start.41 = (f32[512]{0:T(512)S(1)}, f32[512]{0:T(512)}, u32[]{:S(2)}) copy-start(f32[512]{0:T(512)} %get-tuple-element.1340) | copy-start | bytes 6148
  1534.8 5.4 copy-start.25
  1540.2 1.9 copy-start.24
  1653.1 12.3 copy-start.1
  (9 other events, 10.4 us)
Sparse Core Ops, SparseCore 0:
  9.6 49.5 all-gather.12
  60.8 45.6 all-gather.8
  109.0 51.3 all-gather.16
  162.6 52.5 all-gather.18
  217.5 87.4 all-gather.10
  307.3 87.4 all-gather.14
  845.0 205.3 reduce-scatter.23
  1053.4 52.5 reduce-scatter.21
  1109.0 35.1 reduce-scatter.13
  1147.0 65.6 reduce-scatter.15
  1215.7 65.6 reduce-scatter.17
  1284.3 65.6 reduce-scatter.19
  1353.0 70.0 reduce-scatter.11
  1425.6 109.1 all-reduce.8
  1536.3 116.7 all-gather.20
